TPU v7x, 32 devices: a whole 2x2x4 slice. The times are simulated.
32 devices in a mesh: inter: 16 (over z, y, x), intra: 2 (over core).
Axes of the slice: x: 2, y: 2, z: 4, core: 2. Of those that a mesh axis runs over, the one named last changes fastest.
Arguments:
- tokens: bfloat16 [2048, 4096], P('inter', 'intra'), may hold values from -6 to 6
- gate_codes: bfloat16 [7168, 4096], P(('intra', 'inter')), may hold values from -127 to 127
- gate_scales: float32 [7168, 16], P(('intra', 'inter')), may hold values from 0.0001 to 0.0005
- up_codes: bfloat16 [7168, 4096], P(('intra', 'inter')), may hold values from -127 to 127
- up_scales: float32 [7168, 16], P(('intra', 'inter')), may hold values from 0.0001 to 0.0005
- cotangent: bfloat16 [2048, 7168], P('inter', 'intra'), may hold values from -6 to 6
Outputs:
- hidden: bfloat16 [2048, 7168], P('inter', 'intra')
- token_grad: bfloat16 [2048, 4096], P('inter', 'intra')
- gate_grad: float32 [7168, 4096], P(('intra', 'inter'))
- up_grad: float32 [7168, 4096], P(('intra', 'inter'))
All inputs are finite; a program needn't handle non-finite values.
Results may differ from a plain program's by a relative error of at most 0.02.
Values may be sent and summed in bfloat16 or wider, within the bound.
A program may use at most 384 MiB of HBM per device.

v0:
```python
import jax
import jax.numpy as jnp
from jax import lax
from jax.sharding import PartitionSpec as P


def dequantize(codes, scales):
    rows, width = codes.shape
    blocks = scales.shape[1]
    step = width // blocks
    parts = [
        codes[:, b * step : (b + 1) * step].astype(jnp.float32) * scales[:, b : b + 1]
        for b in range(blocks)
    ]
    return jnp.concatenate(parts, axis=1).astype(jnp.bfloat16)


def per_device(tokens, gate_codes, gate_scales, up_codes, up_scales, cotangent):
    groups = lax.axis_size("inter")
    mine = lax.all_gather(tokens, "inter", axis=0, tiled=True)
    whole = lax.all_gather(mine, "intra", axis=0, tiled=False)
    slabs, count, wide = whole.shape
    back = lax.all_to_all(cotangent, "inter", split_axis=1, concat_axis=0, tiled=True)
    w_gate = dequantize(gate_codes, gate_scales)
    w_up = dequantize(up_codes, up_scales)

    def forward(weights):
        total = None
        for s in range(slabs):
            term = lax.dot_general(
                whole[s],
                weights[:, s * wide : (s + 1) * wide],
                (((1,), (1,)), ((), ())),
                preferred_element_type=jnp.float32,
            )
            total = term if total is None else total + term
        return total

    gate = forward(w_gate)
    up = forward(w_up)
    sig = jax.nn.sigmoid(gate)
    act = gate * sig
    hidden = (act * up).astype(jnp.bfloat16)
    back = back.astype(jnp.float32)
    d_up = (back * act).astype(jnp.bfloat16)
    d_gate = (back * up * sig * (1.0 + gate * (1.0 - sig))).astype(jnp.bfloat16)
    hidden = lax.all_to_all(hidden, "inter", split_axis=0, concat_axis=1, tiled=True)
    partial_sum = jnp.dot(d_gate, w_gate, preferred_element_type=jnp.float32)
    partial_sum = partial_sum + jnp.dot(d_up, w_up, preferred_element_type=jnp.float32)
    partial_sum = lax.psum_scatter(
        partial_sum.astype(jnp.bfloat16), "intra", scatter_dimension=1, tiled=True
    )
    token_grad = lax.psum_scatter(partial_sum, "inter", scatter_dimension=0, tiled=True)

    def rows_grad(d_rows):
        terms = [
            lax.dot_general(
                d_rows, whole[s], (((0,), (0,)), ((), ())), preferred_element_type=jnp.float32
            )
            for s in range(slabs)
        ]
        return jnp.concatenate(terms, axis=1) / groups

    return (hidden, token_grad, rows_grad(d_gate), rows_grad(d_up))


def solution(mesh):
    return jax.shard_map(
        per_device,
        mesh=mesh,
        in_specs=(
            P("inter", "intra"),
            P(("intra", "inter"), None),
            P(("intra", "inter"), None),
            P(("intra", "inter"), None),
            P(("intra", "inter"), None),
            P("inter", "intra"),
        ),
        out_specs=(
            P("inter", "intra"),
            P("inter", "intra"),
            P(("intra", "inter"), None),
            P(("intra", "inter"), None),
        ),
        check_vma=False,
    )
```

profile of v0, /device:TPU:26, one launch (start us, length us, event | category | flops | bytes accessed | tf_op | source)
XLA Modules:
  0.0 465.3 jit_solution(1570176110932852104)
XLA Ops:
  7.9 114.0 %all-gather.4.cloned.1.call-done = bf16[2048,2048]{1,0:T(8,128)(2,1)} async-done(((bf16[128,2048]{1,0:T(8,128)(2,1)}), bf16[2048,2048]{1,0:T(8,128)(2,1)}) %all-gather.4.cloned.1.call-update) | async-done | bytes 8388624 | tf_op jit(solution)/shard_map/all_gather | solution.py:20
  124.4 6.3 %all-to-all-start.1 = ((bf16[128,16,224]{0,2,1:T(8,128)(2,1)}), bf16[128,16,224]{0,2,1:T(8,128)(2,1)S(1)}, u32[]{:S(2)}, u32[]{:S(2)}) async-start(bf16[128,16,224]{0,2,1:T(8,128)(2,1)} %bitcast.36), calls=%async_computation.1 | async-start | bytes 1835008 | tf_op jit(solution)/shard_map/all_to_all | solution.py:23
  141.2 1.7 constant_dynamic-update-slice_fusion.47
  143.0 1.7 constant_dynamic-update-slice_fusion.46
  144.7 1.7 constant_dynamic-update-slice_fusion.45
  146.3 1.6 constant_dynamic-update-slice_fusion.44
  148.0 1.6 constant_dynamic-update-slice_fusion.43
  151.3 1.6 constant_dynamic-update-slice_fusion.41
  152.9 1.6 constant_dynamic-update-slice_fusion.40
  154.6 1.8 constant_dynamic-update-slice_fusion.39
  164.3 1.7 constant_dynamic-update-slice_fusion.38
  166.0 1.7 constant_dynamic-update-slice_fusion.37
  167.7 1.7 constant_dynamic-update-slice_fusion.36
  169.4 1.7 constant_dynamic-update-slice_fusion.35
  171.0 1.7 constant_dynamic-update-slice_fusion.34
  172.7 1.7 constant_dynamic-update-slice_fusion.33
  174.4 1.7 constant_dynamic-update-slice_fusion.32
  176.1 7.7 %fusion.2 = f32[224,2048]{1,0:T(8,128)} fusion(bf16[224,2048]{1,0:T(8,128)(2,1)} %copy-done.7, bf16[4096,2048]{1,0:T(8,128)(2,1)} %all-gather.6.cloned.1.call-done), kind=kOutput, calls=%fused_computation.3 | convolution fusion | flops 1879048192 | bytes 11141120 | tf_op jit(solution)/shard_map/dot_general | solution.py:30
  183.8 6.7 %fusion.4 = f32[224,2048]{1,0:T(8,128)S(1)} fusion(bf16[224,2048]{1,0:T(8,128)(2,1)} %get-tuple-element.44, bf16[4096,2048]{1,0:T(8,128)(2,1)} %all-gather.6.cloned.1.call-done), kind=kOutput, calls=%fused_computation.5 | convolution fusion | flops 1879048192 | bytes 11141120 | tf_op jit(solution)/shard_map/dot_general | solution.py:30
  190.5 3.9 fusion.19
  195.3 9.3 %fusion.31 = (bf16[2048,224]{0,1:T(8,128)(2,1)S(1)}, bf16[2048,224]{0,1:T(8,128)(2,1)S(1)}, bf16[28,16,8,128]{3,2,1,0:T(8,128)(2,1)}) fusion(f32[2048,224]{0,1:T(8,128)} %fusion.19, f32[224,2048]{1,0:T(8,128)} %fusion.2, bf16[224,2048]{1,0:T(8,128)(2,1)} %copy-done.8, bf16[4096,2048]{1,0:T(8,128)(2,1)} %all-gather.6.cloned.1.call-done, ...), kind=kOutput, calls=%fused_computation.28 | convolution fusion | flops 1886846976 | bytes 16646144 | tf_op jit(solution)/shard_map/dot_general | solution.py:30
  204.6 15.0 %fusion.38 = f32[2048,4096]{1,0:T(8,128)} fusion(bf16[2048,224]{0,1:T(8,128)(2,1)S(1)} %get-tuple-element.9, bf16[224,4096]{1,0:T(8,128)(2,1)} %get-tuple-element.43), kind=kOutput, calls=%fused_computation.133 | convolution fusion | flops 3758096384 | bytes 36306944 | tf_op jit(solution)/shard_map/dot_general | solution.py:48
  219.6 16.9 %add_convert_fusion = bf16[2048,4096]{1,0:T(8,128)(2,1)} fusion(f32[2048,4096]{1,0:T(8,128)} %fusion.38, bf16[2048,224]{0,1:T(8,128)(2,1)S(1)} %get-tuple-element.8, bf16[224,4096]{1,0:T(8,128)(2,1)S(1)} %get-tuple-element.11), kind=kOutput, calls=%fused_computation | convolution fusion | flops 3774873600 | bytes 53084160 | tf_op jit(solution)/shard_map/dot_general | solution.py:49
  236.6 26.3 %reduce-scatter.3.cloned.1.call-done = bf16[2048,2048]{1,0:T(8,128)(2,1)} async-done(((bf16[2048,4096]{1,0:T(8,128)(2,1)}), bf16[2048,2048]{1,0:T(8,128)(2,1)}) %reduce-scatter.3.cloned.1.call-update) | async-done | bytes 8388624 | tf_op jit(solution)/shard_map/reduce_scatter | solution.py:50
  265.1 6.9 %all-to-all-start = ((bf16[16,128,224]{1,2,0:T(8,128)(2,1)}), bf16[16,128,224]{1,2,0:T(8,128)(2,1)S(1)}, u32[]{:S(2)}, u32[]{:S(2)}) async-start(bf16[16,128,224]{1,2,0:T(8,128)(2,1)} %bitcast.73), calls=%async_computation | async-start | bytes 1835008 | tf_op jit(solution)/shard_map/all_to_all | solution.py:47
  272.1 5.9 %fusion.6 = f32[224,2048]{1,0:T(8,128)S(1)} fusion(bf16[2048,224]{0,1:T(8,128)(2,1)S(1)} %copy-done.4, bf16[4096,2048]{1,0:T(8,128)(2,1)} %all-gather.6.cloned.1.call-done), kind=kOutput, calls=%fused_computation.7 | convolution fusion | flops 1879048192 | bytes 11141120 | tf_op jit(solution)/shard_map/dot_general | solution.py:57
  278.0 5.6 %fusion.14 = f32[224,2048]{1,0:T(8,128)S(1)} fusion(bf16[2048,224]{0,1:T(8,128)(2,1)S(1)} %copy-done.4, bf16[4096,2048]{1,0:T(8,128)(2,1)} %all-gather.6.cloned.1.call-done), kind=kOutput, calls=%fused_computation.15 | convolution fusion | flops 1879048192 | bytes 11141120 | tf_op jit(solution)/shard_map/dot_general | solution.py:57
  283.8 2.1 fusion
  285.9 2.1 fusion.8
  288.1 3.5 maximum_multiply_fusion
  291.6 14.6 %all-to-all-done = bf16[16,128,224]{1,2,0:T(8,128)(2,1)S(1)} async-done(((bf16[16,128,224]{1,2,0:T(8,128)(2,1)}), bf16[16,128,224]{1,2,0:T(8,128)(2,1)S(1)}, u32[]{:S(2)}, u32[]{:S(2)}) %all-to-all-start) | async-done | bytes 917536 | tf_op jit(solution)/shard_map/all_to_all | solution.py:47
  307.5 151.2 %reduce-scatter.5.cloned.1.call-done = bf16[128,2048]{1,0:T(8,128)(2,1)} async-done(((bf16[2048,2048]{1,0:T(8,128)(2,1)}), bf16[128,2048]{1,0:T(8,128)(2,1)}) %reduce-scatter.5.cloned.1.call-update) | async-done | bytes 524304 | tf_op jit(solution)/shard_map/reduce_scatter | solution.py:53
  (65 shorter events, 27.9 us)
Async XLA Ops:
  7.2 114.8 %all-gather.4.cloned.1.call-start = ((), (), s32[]{:S(2)}) async-start(), calls=%async_computation.4 | async-start | bytes 8912896 | tf_op jit(solution)/shard_map/all_gather | solution.py:20
  7.9 168.2 %all-gather.6.cloned.1.call-start = ((), (), s32[]{:S(2)}) async-start(), calls=%async_computation.7 | async-start | bytes 25165824 | tf_op jit(solution)/shard_map/all_gather | solution.py:21
  122.0 1.2 copy-start
  123.1 7.6 %copy-start.5 = (f32[224,16]{0,1:T(8,128)S(1)}, f32[224,16]{0,1:T(8,128)}, u32[]{:S(2)}) copy-start(f32[224,16]{0,1:T(8,128)} %param.8) | copy-start | bytes 43012
  123.1 7.6 %copy-start.6 = (f32[224,16]{0,1:T(8,128)S(1)}, f32[224,16]{0,1:T(8,128)}, u32[]{:S(2)}) copy-start(f32[224,16]{0,1:T(8,128)} %param.10) | copy-start | bytes 43012
  124.4 70.0 %all-to-all-start.1 = ((bf16[128,16,224]{0,2,1:T(8,128)(2,1)}), bf16[128,16,224]{0,2,1:T(8,128)(2,1)S(1)}, u32[]{:S(2)}, u32[]{:S(2)}) async-start(bf16[128,16,224]{0,2,1:T(8,128)(2,1)} %bitcast.36), calls=%async_computation.1 | async-start | bytes 1835008 | tf_op jit(solution)/shard_map/all_to_all | solution.py:23
  130.7 132.2 %reduce-scatter.3.cloned.1.call-start = ((), (), s32[]{:S(2)}) async-start(), calls=%async_computation.5 | async-start | bytes 25165824 | tf_op jit(solution)/shard_map/reduce_scatter | solution.py:50
  139.2 1.0 copy-start.8
  154.6 14.8 %copy-start.9 = (bf16[224,2048]{1,0:T(8,128)(2,1)}, bf16[224,2048]{1,0:T(8,128)(2,1)S(1)}, u32[]{:S(2)}) copy-start(bf16[224,2048]{1,0:T(8,128)(2,1)S(1)} %get-tuple-element.60) | copy-start | bytes 2752516
  163.4 0.9 copy-start.7
  176.1 14.4 %copy-start.11 = (bf16[4096,2048]{1,0:T(8,128)(2,1)S(1)}, bf16[4096,2048]{1,0:T(8,128)(2,1)}, u32[]{:S(2)}) copy-start(bf16[4096,2048]{1,0:T(8,128)(2,1)} %all-gather.6.cloned.1.call-done) | copy-start | bytes 50331652
  183.8 6.7 %copy-start.10 = (bf16[224,2048]{1,0:T(8,128)(2,1)S(1)}, bf16[224,2048]{1,0:T(8,128)(2,1)}, u32[]{:S(2)}) copy-start(bf16[224,2048]{1,0:T(8,128)(2,1)} %copy-done.9) | copy-start | bytes 2752516
  194.4 0.9 copy-start.1
  204.6 15.0 %copy-start.3 = (bf16[2048,224]{0,1:T(8,128)(2,1)}, bf16[2048,224]{0,1:T(8,128)(2,1)S(1)}, u32[]{:S(2)}) copy-start(bf16[2048,224]{0,1:T(8,128)(2,1)S(1)} %get-tuple-element.8) | copy-start | bytes 2752516
  236.5 222.2 %reduce-scatter.5.cloned.1.call-start = ((), (), s32[]{:S(2)}) async-start(), calls=%async_computation.6 | async-start | bytes 8912896 | tf_op jit(solution)/shard_map/reduce_scatter | solution.py:53
  262.9 1.2 copy-start.2
  264.0 8.0 %copy-start.4 = (bf16[2048,224]{0,1:T(8,128)(2,1)S(1)}, bf16[2048,224]{0,1:T(8,128)(2,1)}, u32[]{:S(2)}) copy-start(bf16[2048,224]{0,1:T(8,128)(2,1)} %copy-done.3) | copy-start | bytes 2752516
  265.1 41.1 %all-to-all-start = ((bf16[16,128,224]{1,2,0:T(8,128)(2,1)}), bf16[16,128,224]{1,2,0:T(8,128)(2,1)S(1)}, u32[]{:S(2)}, u32[]{:S(2)}) async-start(bf16[16,128,224]{1,2,0:T(8,128)(2,1)} %bitcast.73), calls=%async_computation | async-start | bytes 1835008 | tf_op jit(solution)/shard_map/all_to_all | solution.py:47
  272.1 11.5 %slice-start = ((s8[16777216]{0:T(1024)(128)(4,1)}), s8[4194304]{0:T(1024)(128)(4,1)S(1)}, s32[]{:S(2)}) async-start(s8[16777216]{0:T(1024)(128)(4,1)} %bitcast.107), calls=%async_computation.8 | async-start | bytes 8388608
  272.1 11.5 %slice-start.1 = ((s8[16777216]{0:T(1024)(128)(4,1)}), s8[4194304]{0:T(1024)(128)(4,1)S(1)}, s32[]{:S(2)}) async-start(s8[16777216]{0:T(1024)(128)(4,1)} %bitcast.107), calls=%async_computation.9 | async-start | bytes 8388608
  277.9 5.6 %slice-start.2 = ((s8[16777216]{0:T(1024)(128)(4,1)}), s8[4194304]{0:T(1024)(128)(4,1)S(1)}, s32[]{:S(2)}) async-start(s8[16777216]{0:T(1024)(128)(4,1)} %bitcast.107), calls=%async_computation.10 | async-start | bytes 8388608
  278.0 5.8 %slice-start.3 = ((s8[16777216]{0:T(1024)(128)(4,1)}), s8[4194304]{0:T(1024)(128)(4,1)S(1)}, s32[]{:S(2)}) async-start(s8[16777216]{0:T(1024)(128)(4,1)} %bitcast.107), calls=%async_computation.11 | async-start | bytes 8388608
Sparse Core Ops, SparseCore 0:
  10.7 111.1 all-gather.3
  123.5 30.5 all-gather.5
  236.6 26.1 reduce-scatter.2
  265.6 193.1 reduce-scatter.4
where the time goes:
time: 467 us; the launch traced here: 465 us
  waiting for transfers between devices  307 us (66%)
  matrix products  75.2 us (16%)
  other arithmetic  46.8 us (10%)
  between operations  14.1 us (3%)
  starting transfers between devices  13.3 us (3%)
  local copies, waits for them, and re-layouts  8.98 us (2%)
    reduce_scatter x1, waiting for transfers between devices, per_device(): lax.psum_scatter(partial_sum, 'inter', scatter_dimension=0, tiled=True)  151 us
    all_gather x1, waiting for transfers between devices, per_device(): mine = lax.all_gather(tokens, 'inter', axis=0, tiled=True)  114 us
    unnamed x31, other arithmetic  40.6 us
    dot_general x4, matrix products, forward(): lax.dot_general(whole[s], weights[:, s * wide:(s + 1) * wide], (((1,), (1...  27.5 us
    reduce_scatter x1, waiting for transfers between devices, per_device(): lax.psum_scatter(partial_sum.astype(jnp.bfloat16), 'intra', scatter_dimen...  26.3 us
    dot_general x1, matrix products, per_device(): jnp.dot(d_up, w_up, preferred_element_type=jnp.float32)  16.9 us
    dot_general x4, matrix products, rows_grad(): lax.dot_general(d_rows, whole[s], (((0,), (0,)), ((), ())), preferred_ele...  15.7 us
    dot_general x1, matrix products, per_device(): partial_sum = jnp.dot(d_gate, w_gate, preferred_element_type=jnp.float32)  15 us
  transfers between devices with their start and end apart: 6, of which 4 were waited for; matrix products, arithmetic and copies ran while one was open for 18% of the time, Pallas kernels for 0%

commit v1 on v0

--- a/solution.py
+++ b/solution.py
@@ -2,6 +2,7 @@
 import jax.numpy as jnp
 from jax import lax
 from jax.sharding import PartitionSpec as P
+from jax.lax import axis_index, axis_size, ppermute
 
 
 def dequantize(codes, scales):
@@ -16,8 +17,34 @@
 
 
 def per_device(tokens, gate_codes, gate_scales, up_codes, up_scales, cotangent):
+
+    def bind_sheets(vector):
+        oldest = axis_size("inter")
+        tile_out, x_now, piece_next = (oldest, axis_index("inter"), vector.shape[0])
+        history = []
+        for jj in range(tile_out):
+            history.append((jj, (jj + 1) % tile_out))
+        lanes = []
+        for jj in range(tile_out):
+            lanes.append((jj, (jj - 1) % tile_out))
+        top = jnp.zeros((*vector.shape[:0], tile_out * piece_next, *vector.shape[1:]), vector.dtype)
+        top = lax.dynamic_update_slice_in_dim(top, vector, x_now * piece_next, axis=0)
+        mixed_arr = z = vector
+        val = tile_out // 2
+        for num in range(1, val + 1):
+            mixed_arr = ppermute(mixed_arr, axis_name="inter", perm=history)
+            top = lax.dynamic_update_slice_in_dim(
+                top, mixed_arr, (x_now - num) % tile_out * piece_next, axis=0
+            )
+            if num < tile_out - val:
+                z = ppermute(z, axis_name="inter", perm=lanes)
+                top = lax.dynamic_update_slice_in_dim(
+                    top, z, (x_now + num) % tile_out * piece_next, axis=0
+                )
+        return top
+
     groups = lax.axis_size("inter")
-    mine = lax.all_gather(tokens, "inter", axis=0, tiled=True)
+    mine = bind_sheets(tokens)
     whole = lax.all_gather(mine, "intra", axis=0, tiled=False)
     slabs, count, wide = whole.shape
     back = lax.all_to_all(cotangent, "inter", split_axis=1, concat_axis=0, tiled=True)

time: 467 us -> 546 us (1.17)
  waiting for transfers between devices: 307 us -> 348 us
  starting transfers between devices: 13.3 us -> 34.2 us
  local copies, waits for them, and re-layouts: 8.98 us -> 28.9 us
    ppermute x0 -> x15, waiting for transfers between devices: none -> 158 us  [the longest x8 96 us: bind_sheets(): mixed_arr = ppermute(mixed_arr, axis_name='inter', perm=history)]
    all_gather x1 -> x0, waiting for transfers between devices: 114 us -> none  [per_device(): mine = lax.all_gather(tokens, 'inter', axis=0, tiled=True)]
    dynamic_update_slice x0 -> x16, local copies, waits for them, and re-layouts: none -> 13.5 us  [the longest x8 6.7 us: bind_sheets(): lax.dynamic_update_slice_in_dim(top, mixed_arr, (x_now - num) % tile_out...]
    all_to_all x1, starting transfers between devices: 6.25 us -> 17.4 us  [per_device(): lax.all_to_all(cotangent, 'inter', split_axis=1, concat_axis=0, tiled=True)]
    ppermute x0 -> x15, starting transfers between devices: none -> 9.52 us  [the longest x8 8.92 us: bind_sheets(): mixed_arr = ppermute(mixed_arr, axis_name='inter', perm=history)]
  transfers between devices with their start and end apart: 6 -> 20, of which waited for: 4 -> 17; matrix products, arithmetic and copies ran while one was open for 18% -> 17% of each run, Pallas kernels for 0% -> 0%
where the time goes in v1:
time: 546 us; the launch traced here: 544 us
  waiting for transfers between devices  348 us (64%)
  matrix products  72.7 us (13%)
  other arithmetic  46.7 us (9%)
  starting transfers between devices  34.2 us (6%)
  local copies, waits for them, and re-layouts  28.9 us (5%)
  between operations  14.1 us (3%)
    reduce_scatter x1, waiting for transfers between devices, per_device(): lax.psum_scatter(partial_sum, 'inter', scatter_dimension=0, tiled=True)  149 us
    ppermute x8, waiting for transfers between devices, bind_sheets(): mixed_arr = ppermute(mixed_arr, axis_name='inter', perm=history)  96 us
    ppermute x7, waiting for transfers between devices, bind_sheets(): z = ppermute(z, axis_name='inter', perm=lanes)  61.8 us
    unnamed x31, other arithmetic  40.4 us
    reduce_scatter x1, waiting for transfers between devices, per_device(): lax.psum_scatter(partial_sum.astype(jnp.bfloat16), 'intra', scatter_dimen...  26.3 us
    dot_general x4, matrix products, forward(): lax.dot_general(whole[s], weights[:, s * wide:(s + 1) * wide], (((1,), (1...  24.9 us
    all_to_all x1, starting transfers between devices, per_device(): lax.all_to_all(cotangent, 'inter', split_axis=1, concat_axis=0, tiled=True)  17.4 us
    dot_general x1, matrix products, per_device(): jnp.dot(d_up, w_up, preferred_element_type=jnp.float32)  16.9 us
  transfers between devices with their start and end apart: 20, of which 17 were waited for; matrix products, arithmetic and copies ran while one was open for 17% of the time, Pallas kernels for 0%

profile of v1, /device:TPU:26, one launch (start us, length us, event | category | flops | bytes accessed | tf_op | source)
XLA Modules:
  0.0 544.5 jit_solution(3375337935402846439)
XLA Ops:
  7.8 2.4 collective-permute-start
  10.2 4.4 all_gather.38
  15.5 7.7 %collective-permute-done.1 = bf16[128,2048]{1,0:T(8,128)(2,1)S(1)} collective-permute-done((bf16[128,2048]{1,0:T(8,128)(2,1)}, bf16[128,2048]{1,0:T(8,128)(2,1)S(1)}, u32[]{:S(2)}, u32[]{:S(2)}) %collective-permute-start.1) | collective-permute-done | bytes 524320 | tf_op jit(solution)/shard_map/ppermute | solution.py:40
  23.2 10.1 %collective-permute-done = bf16[128,2048]{1,0:T(8,128)(2,1)S(1)} collective-permute-done((bf16[128,2048]{1,0:T(8,128)(2,1)}, bf16[128,2048]{1,0:T(8,128)(2,1)S(1)}, u32[]{:S(2)}, u32[]{:S(2)}) %collective-permute-start) | collective-permute-done | bytes 524320 | tf_op jit(solution)/shard_map/ppermute | solution.py:35
  36.6 10.0 %collective-permute-done.3 = bf16[128,2048]{1,0:T(8,128)(2,1)S(1)} collective-permute-done((bf16[128,2048]{1,0:T(8,128)(2,1)S(1)}, bf16[128,2048]{1,0:T(8,128)(2,1)S(1)}, u32[]{:S(2)}, u32[]{:S(2)}) %collective-permute-start.3) | collective-permute-done | bytes 524320 | tf_op jit(solution)/shard_map/ppermute | solution.py:40
  46.6 10.7 %collective-permute-done.2 = bf16[128,2048]{1,0:T(8,128)(2,1)S(1)} collective-permute-done((bf16[128,2048]{1,0:T(8,128)(2,1)S(1)}, bf16[128,2048]{1,0:T(8,128)(2,1)S(1)}, u32[]{:S(2)}, u32[]{:S(2)}) %collective-permute-start.2) | collective-permute-done | bytes 524320 | tf_op jit(solution)/shard_map/ppermute | solution.py:35
  59.6 11.1 %collective-permute-done.5 = bf16[128,2048]{1,0:T(8,128)(2,1)S(1)} collective-permute-done((bf16[128,2048]{1,0:T(8,128)(2,1)S(1)}, bf16[128,2048]{1,0:T(8,128)(2,1)S(1)}, u32[]{:S(2)}, u32[]{:S(2)}) %collective-permute-start.5) | collective-permute-done | bytes 524320 | tf_op jit(solution)/shard_map/ppermute | solution.py:40
  70.7 10.8 %collective-permute-done.4 = bf16[128,2048]{1,0:T(8,128)(2,1)S(1)} collective-permute-done((bf16[128,2048]{1,0:T(8,128)(2,1)S(1)}, bf16[128,2048]{1,0:T(8,128)(2,1)S(1)}, u32[]{:S(2)}, u32[]{:S(2)}) %collective-permute-start.4) | collective-permute-done | bytes 524320 | tf_op jit(solution)/shard_map/ppermute | solution.py:35
  83.6 11.1 %collective-permute-done.7 = bf16[128,2048]{1,0:T(8,128)(2,1)S(1)} collective-permute-done((bf16[128,2048]{1,0:T(8,128)(2,1)S(1)}, bf16[128,2048]{1,0:T(8,128)(2,1)S(1)}, u32[]{:S(2)}, u32[]{:S(2)}) %collective-permute-start.7) | collective-permute-done | bytes 524320 | tf_op jit(solution)/shard_map/ppermute | solution.py:40
  94.7 11.1 %collective-permute-done.6 = bf16[128,2048]{1,0:T(8,128)(2,1)S(1)} collective-permute-done((bf16[128,2048]{1,0:T(8,128)(2,1)S(1)}, bf16[128,2048]{1,0:T(8,128)(2,1)S(1)}, u32[]{:S(2)}, u32[]{:S(2)}) %collective-permute-start.6) | collective-permute-done | bytes 524320 | tf_op jit(solution)/shard_map/ppermute | solution.py:35
  107.7 11.1 %collective-permute-done.9 = bf16[128,2048]{1,0:T(8,128)(2,1)S(1)} collective-permute-done((bf16[128,2048]{1,0:T(8,128)(2,1)S(1)}, bf16[128,2048]{1,0:T(8,128)(2,1)S(1)}, u32[]{:S(2)}, u32[]{:S(2)}) %collective-permute-start.9) | collective-permute-done | bytes 524320 | tf_op jit(solution)/shard_map/ppermute | solution.py:40
  118.8 11.4 %collective-permute-done.8 = bf16[128,2048]{1,0:T(8,128)(2,1)S(1)} collective-permute-done((bf16[128,2048]{1,0:T(8,128)(2,1)S(1)}, bf16[128,2048]{1,0:T(8,128)(2,1)S(1)}, u32[]{:S(2)}, u32[]{:S(2)}) %collective-permute-start.8) | collective-permute-done | bytes 524320 | tf_op jit(solution)/shard_map/ppermute | solution.py:35
  132.0 10.8 %collective-permute-done.11 = bf16[128,2048]{1,0:T(8,128)(2,1)S(1)} collective-permute-done((bf16[128,2048]{1,0:T(8,128)(2,1)S(1)}, bf16[128,2048]{1,0:T(8,128)(2,1)S(1)}, u32[]{:S(2)}, u32[]{:S(2)}) %collective-permute-start.11) | collective-permute-done | bytes 524320 | tf_op jit(solution)/shard_map/ppermute | solution.py:40
  142.8 16.4 %collective-permute-done.10 = bf16[128,2048]{1,0:T(8,128)(2,1)S(1)} collective-permute-done((bf16[128,2048]{1,0:T(8,128)(2,1)S(1)}, bf16[128,2048]{1,0:T(8,128)(2,1)S(1)}, u32[]{:S(2)}, u32[]{:S(2)}) %collective-permute-start.10) | collective-permute-done | bytes 524320 | tf_op jit(solution)/shard_map/ppermute | solution.py:35
  160.9 17.8 %collective-permute-done.12 = bf16[128,2048]{1,0:T(8,128)(2,1)S(1)} collective-permute-done((bf16[128,2048]{1,0:T(8,128)(2,1)S(1)}, bf16[128,2048]{1,0:T(8,128)(2,1)S(1)}, u32[]{:S(2)}, u32[]{:S(2)}) %collective-permute-start.12) | collective-permute-done | bytes 524320 | tf_op jit(solution)/shard_map/ppermute | solution.py:35
  178.7 3.5 collective-permute-start.14
  183.8 7.8 %collective-permute-done.14 = bf16[128,2048]{1,0:T(8,128)(2,1)S(1)} collective-permute-done((bf16[128,2048]{1,0:T(8,128)(2,1)S(1)}, bf16[128,2048]{1,0:T(8,128)(2,1)S(1)}, u32[]{:S(2)}, u32[]{:S(2)}) %collective-permute-start.14) | collective-permute-done | bytes 524320 | tf_op jit(solution)/shard_map/ppermute | solution.py:35
  194.9 17.4 %all-to-all-start.1 = ((bf16[128,16,224]{0,2,1:T(8,128)(2,1)}), bf16[128,16,224]{0,2,1:T(8,128)(2,1)S(1)}, u32[]{:S(2)}, u32[]{:S(2)}) async-start(bf16[128,16,224]{0,2,1:T(8,128)(2,1)} %bitcast.52), calls=%async_computation.1 | async-start | bytes 1835008 | tf_op jit(solution)/shard_map/all_to_all | solution.py:50
  257.8 6.4 %fusion.6 = f32[2048,224]{0,1:T(8,128)S(1)} fusion(bf16[224,2048]{1,0:T(8,128)(2,1)} %copy-done.8, bf16[2,2048,2048]{2,1,0:T(8,128)(2,1)} %all-gather.2.cloned.1.call-done), kind=kOutput, calls=%fused_computation.9 | convolution fusion | flops 1879048192 | bytes 11141120 | tf_op jit(solution)/shard_map/dot_general | solution.py:57
  266.2 5.2 fusion.7
  271.4 3.9 fusion.9
  276.2 9.5 %fusion.13 = (bf16[2048,224]{0,1:T(8,128)(2,1)S(1)}, bf16[2048,224]{0,1:T(8,128)(2,1)S(1)}, bf16[28,16,8,128]{3,2,1,0:T(8,128)(2,1)}) fusion(f32[2048,224]{0,1:T(8,128)} %fusion.9, f32[2048,224]{0,1:T(8,128)} %fusion.7, bf16[224,2048]{1,0:T(8,128)(2,1)} %copy-done.11, bf16[2,2048,2048]{2,1,0:T(8,128)(2,1)} %all-gather.2.cloned.1.call-done, ...), kind=kOutput, calls=%fused_computation.20 | convolution fusion | flops 1886846976 | bytes 16646144 | tf_op jit(solution)/shard_map/dot_general | solution.py:57
  285.7 15.0 %fusion.18 = f32[2048,4096]{1,0:T(8,128)} fusion(bf16[2048,224]{0,1:T(8,128)(2,1)S(1)} %get-tuple-element.13, bf16[224,4096]{1,0:T(8,128)(2,1)} %get-tuple-element.47), kind=kOutput, calls=%fused_computation.141 | convolution fusion | flops 3758096384 | bytes 36306944 | tf_op jit(solution)/shard_map/dot_general | solution.py:75
  300.7 16.9 %add_convert_fusion = bf16[2048,4096]{1,0:T(8,128)(2,1)} fusion(f32[2048,4096]{1,0:T(8,128)} %fusion.18, bf16[2048,224]{0,1:T(8,128)(2,1)S(1)} %get-tuple-element.12, bf16[224,4096]{1,0:T(8,128)(2,1)S(1)} %get-tuple-element.15), kind=kOutput, calls=%fused_computation | convolution fusion | flops 3774873600 | bytes 53084160 | tf_op jit(solution)/shard_map/dot_general | solution.py:76
  317.7 26.3 %reduce-scatter.3.cloned.1.call-done = bf16[2048,2048]{1,0:T(8,128)(2,1)} async-done(((bf16[2048,4096]{1,0:T(8,128)(2,1)}), bf16[2048,2048]{1,0:T(8,128)(2,1)}) %reduce-scatter.3.cloned.1.call-update) | async-done | bytes 8388624 | tf_op jit(solution)/shard_map/reduce_scatter | solution.py:77
  346.3 6.9 %all-to-all-start = ((bf16[16,128,224]{1,2,0:T(8,128)(2,1)}), bf16[16,128,224]{1,2,0:T(8,128)(2,1)S(1)}, u32[]{:S(2)}, u32[]{:S(2)}) async-start(bf16[16,128,224]{1,2,0:T(8,128)(2,1)} %bitcast.117), calls=%async_computation | async-start | bytes 1835008 | tf_op jit(solution)/shard_map/all_to_all | solution.py:74
  353.2 5.9 %fusion.4 = f32[224,2048]{1,0:T(8,128)S(1)} fusion(bf16[2048,224]{0,1:T(8,128)(2,1)S(1)} %copy-done.4, bf16[2,2048,2048]{2,1,0:T(8,128)(2,1)} %all-gather.2.cloned.1.call-done), kind=kOutput, calls=%fused_computation.7 | convolution fusion | flops 1879048192 | bytes 11141120 | tf_op jit(solution)/shard_map/dot_general | solution.py:84
  359.2 5.6 %fusion = f32[224,2048]{1,0:T(8,128)S(1)} fusion(bf16[2048,224]{0,1:T(8,128)(2,1)S(1)} %copy-done.4, bf16[2,2048,2048]{2,1,0:T(8,128)(2,1)} %all-gather.2.cloned.1.call-done), kind=kOutput, calls=%fused_computation.3 | convolution fusion | flops 1879048192 | bytes 11141120 | tf_op jit(solution)/shard_map/dot_general | solution.py:84
  367.1 2.1 fusion.1
  369.3 3.5 maximum_multiply_fusion
  372.8 14.6 %all-to-all-done = bf16[16,128,224]{1,2,0:T(8,128)(2,1)S(1)} async-done(((bf16[16,128,224]{1,2,0:T(8,128)(2,1)}), bf16[16,128,224]{1,2,0:T(8,128)(2,1)S(1)}, u32[]{:S(2)}, u32[]{:S(2)}) %all-to-all-start) | async-done | bytes 917536 | tf_op jit(solution)/shard_map/all_to_all | solution.py:74
  388.7 149.3 %reduce-scatter.5.cloned.1.call-done = bf16[128,2048]{1,0:T(8,128)(2,1)} async-done(((bf16[2048,2048]{1,0:T(8,128)(2,1)}), bf16[128,2048]{1,0:T(8,128)(2,1)}) %reduce-scatter.5.cloned.1.call-update) | async-done | bytes 524304 | tf_op jit(solution)/shard_map/reduce_scatter | solution.py:80
  (111 shorter events, 73.8 us)
Async XLA Ops:
  7.2 250.6 %all-gather.2.cloned.1.call-start = ((), (), s32[]{:S(2)}) async-start(), calls=%async_computation.4 | async-start | bytes 25165824 | tf_op jit(solution)/shard_map/all_gather | solution.py:48
  7.2 16.0 %collective-permute-start.1 = (bf16[128,2048]{1,0:T(8,128)(2,1)}, bf16[128,2048]{1,0:T(8,128)(2,1)S(1)}, u32[]{:S(2)}, u32[]{:S(2)}) collective-permute-start(bf16[128,2048]{1,0:T(8,128)(2,1)} %param.6), channel_id=1, source_target_pairs={{0,30},{2,0},{4,2},{6,4},{8,6},{10,8},{12,10},{14,12},{16,14},{18,... | collective-permute-start | bytes 1572872 | tf_op jit(solution)/shard_map/ppermute | solution.py:40
  7.8 25.5 %collective-permute-start = (bf16[128,2048]{1,0:T(8,128)(2,1)}, bf16[128,2048]{1,0:T(8,128)(2,1)S(1)}, u32[]{:S(2)}, u32[]{:S(2)}) collective-permute-start(bf16[128,2048]{1,0:T(8,128)(2,1)} %param.6), channel_id=1, source_target_pairs={{0,2},{2,4},{4,6},{6,8},{8,10},{10,12},{12,14},{14,16},{16,18},{18... | collective-permute-start | bytes 1572872 | tf_op jit(solution)/shard_map/ppermute | solution.py:35
  10.2 4.4 copy-start.5
  23.2 23.5 %collective-permute-start.3 = (bf16[128,2048]{1,0:T(8,128)(2,1)S(1)}, bf16[128,2048]{1,0:T(8,128)(2,1)S(1)}, u32[]{:S(2)}, u32[]{:S(2)}) collective-permute-start(bf16[128,2048]{1,0:T(8,128)(2,1)S(1)} %collective-permute-done.1), channel_id=1, source_target_pairs={{0,30},{2,0},{4,2},{6,4},{8,6},{10,8},{12,10},{14,12},{16,14},{18,... | collective-permute-start | bytes 1572872 | tf_op jit(solution)/shard_map/ppermute | solution.py:40
  33.2 24.0 %collective-permute-start.2 = (bf16[128,2048]{1,0:T(8,128)(2,1)S(1)}, bf16[128,2048]{1,0:T(8,128)(2,1)S(1)}, u32[]{:S(2)}, u32[]{:S(2)}) collective-permute-start(bf16[128,2048]{1,0:T(8,128)(2,1)S(1)} %collective-permute-done), channel_id=1, source_target_pairs={{0,2},{2,4},{4,6},{6,8},{8,10},{10,12},{12,14},{14,16},{16,18},{18... | collective-permute-start | bytes 1572872 | tf_op jit(solution)/shard_map/ppermute | solution.py:35
  46.6 24.0 %collective-permute-start.5 = (bf16[128,2048]{1,0:T(8,128)(2,1)S(1)}, bf16[128,2048]{1,0:T(8,128)(2,1)S(1)}, u32[]{:S(2)}, u32[]{:S(2)}) collective-permute-start(bf16[128,2048]{1,0:T(8,128)(2,1)S(1)} %collective-permute-done.3), channel_id=1, source_target_pairs={{0,30},{2,0},{4,2},{6,4},{8,6},{10,8},{12,10},{14,12},{16,14},{18,... | collective-permute-start | bytes 1572872 | tf_op jit(solution)/shard_map/ppermute | solution.py:40
  57.3 24.1 %collective-permute-start.4 = (bf16[128,2048]{1,0:T(8,128)(2,1)S(1)}, bf16[128,2048]{1,0:T(8,128)(2,1)S(1)}, u32[]{:S(2)}, u32[]{:S(2)}) collective-permute-start(bf16[128,2048]{1,0:T(8,128)(2,1)S(1)} %collective-permute-done.2), channel_id=1, source_target_pairs={{0,2},{2,4},{4,6},{6,8},{8,10},{10,12},{12,14},{14,16},{16,18},{18... | collective-permute-start | bytes 1572872 | tf_op jit(solution)/shard_map/ppermute | solution.py:35
  70.7 24.0 %collective-permute-start.7 = (bf16[128,2048]{1,0:T(8,128)(2,1)S(1)}, bf16[128,2048]{1,0:T(8,128)(2,1)S(1)}, u32[]{:S(2)}, u32[]{:S(2)}) collective-permute-start(bf16[128,2048]{1,0:T(8,128)(2,1)S(1)} %collective-permute-done.5), channel_id=1, source_target_pairs={{0,30},{2,0},{4,2},{6,4},{8,6},{10,8},{12,10},{14,12},{16,14},{18,... | collective-permute-start | bytes 1572872 | tf_op jit(solution)/shard_map/ppermute | solution.py:40
  81.4 24.4 %collective-permute-start.6 = (bf16[128,2048]{1,0:T(8,128)(2,1)S(1)}, bf16[128,2048]{1,0:T(8,128)(2,1)S(1)}, u32[]{:S(2)}, u32[]{:S(2)}) collective-permute-start(bf16[128,2048]{1,0:T(8,128)(2,1)S(1)} %collective-permute-done.4), channel_id=1, source_target_pairs={{0,2},{2,4},{4,6},{6,8},{8,10},{10,12},{12,14},{14,16},{16,18},{18... | collective-permute-start | bytes 1572872 | tf_op jit(solution)/shard_map/ppermute | solution.py:35
  94.7 24.1 %collective-permute-start.9 = (bf16[128,2048]{1,0:T(8,128)(2,1)S(1)}, bf16[128,2048]{1,0:T(8,128)(2,1)S(1)}, u32[]{:S(2)}, u32[]{:S(2)}) collective-permute-start(bf16[128,2048]{1,0:T(8,128)(2,1)S(1)} %collective-permute-done.7), channel_id=1, source_target_pairs={{0,30},{2,0},{4,2},{6,4},{8,6},{10,8},{12,10},{14,12},{16,14},{18,... | collective-permute-start | bytes 1572872 | tf_op jit(solution)/shard_map/ppermute | solution.py:40
  105.8 24.4 %collective-permute-start.8 = (bf16[128,2048]{1,0:T(8,128)(2,1)S(1)}, bf16[128,2048]{1,0:T(8,128)(2,1)S(1)}, u32[]{:S(2)}, u32[]{:S(2)}) collective-permute-start(bf16[128,2048]{1,0:T(8,128)(2,1)S(1)} %collective-permute-done.6), channel_id=1, source_target_pairs={{0,2},{2,4},{4,6},{6,8},{8,10},{10,12},{12,14},{14,16},{16,18},{18... | collective-permute-start | bytes 1572872 | tf_op jit(solution)/shard_map/ppermute | solution.py:35
  118.8 24.0 %collective-permute-start.11 = (bf16[128,2048]{1,0:T(8,128)(2,1)S(1)}, bf16[128,2048]{1,0:T(8,128)(2,1)S(1)}, u32[]{:S(2)}, u32[]{:S(2)}) collective-permute-start(bf16[128,2048]{1,0:T(8,128)(2,1)S(1)} %collective-permute-done.9), channel_id=1, source_target_pairs={{0,30},{2,0},{4,2},{6,4},{8,6},{10,8},{12,10},{14,12},{16,14},{18,... | collective-permute-start | bytes 1572872 | tf_op jit(solution)/shard_map/ppermute | solution.py:40
  130.2 28.9 %collective-permute-start.10 = (bf16[128,2048]{1,0:T(8,128)(2,1)S(1)}, bf16[128,2048]{1,0:T(8,128)(2,1)S(1)}, u32[]{:S(2)}, u32[]{:S(2)}) collective-permute-start(bf16[128,2048]{1,0:T(8,128)(2,1)S(1)} %collective-permute-done.8), channel_id=1, source_target_pairs={{0,2},{2,4},{4,6},{6,8},{8,10},{10,12},{12,14},{14,16},{16,18},{18... | collective-permute-start | bytes 1572872 | tf_op jit(solution)/shard_map/ppermute | solution.py:35
  142.8 40.2 %collective-permute-start.13 = (bf16[128,2048]{1,0:T(8,128)(2,1)S(1)}, bf16[128,2048]{1,0:T(8,128)(2,1)S(1)}, u32[]{:S(2)}, u32[]{:S(2)}) collective-permute-start(bf16[128,2048]{1,0:T(8,128)(2,1)S(1)} %collective-permute-done.11), channel_id=1, source_target_pairs={{0,30},{2,0},{4,2},{6,4},{8,6},{10,8},{12,10},{14,12},{16,14},{18,... | collective-permute-start | bytes 1572872 | tf_op jit(solution)/shard_map/ppermute | solution.py:40
  159.2 19.5 %collective-permute-start.12 = (bf16[128,2048]{1,0:T(8,128)(2,1)S(1)}, bf16[128,2048]{1,0:T(8,128)(2,1)S(1)}, u32[]{:S(2)}, u32[]{:S(2)}) collective-permute-start(bf16[128,2048]{1,0:T(8,128)(2,1)S(1)} %collective-permute-done.10), channel_id=1, source_target_pairs={{0,2},{2,4},{4,6},{6,8},{8,10},{10,12},{12,14},{14,16},{16,18},{18... | collective-permute-start | bytes 1572872 | tf_op jit(solution)/shard_map/ppermute | solution.py:35
  178.7 13.0 %collective-permute-start.14 = (bf16[128,2048]{1,0:T(8,128)(2,1)S(1)}, bf16[128,2048]{1,0:T(8,128)(2,1)S(1)}, u32[]{:S(2)}, u32[]{:S(2)}) collective-permute-start(bf16[128,2048]{1,0:T(8,128)(2,1)S(1)} %collective-permute-done.12), channel_id=1, source_target_pairs={{0,2},{2,4},{4,6},{6,8},{8,10},{10,12},{12,14},{14,16},{16,18},{18... | collective-permute-start | bytes 1572872 | tf_op jit(solution)/shard_map/ppermute | solution.py:35
  193.7 18.9 %copy-start.6 = (f32[224,16]{0,1:T(8,128)S(1)}, f32[224,16]{0,1:T(8,128)}, u32[]{:S(2)}) copy-start(f32[224,16]{0,1:T(8,128)} %param.8) | copy-start | bytes 43012
  193.7 19.0 %copy-start.7 = (f32[224,16]{0,1:T(8,128)S(1)}, f32[224,16]{0,1:T(8,128)}, u32[]{:S(2)}) copy-start(f32[224,16]{0,1:T(8,128)} %param.10) | copy-start | bytes 43012
  194.9 80.3 %all-to-all-start.1 = ((bf16[128,16,224]{0,2,1:T(8,128)(2,1)}), bf16[128,16,224]{0,2,1:T(8,128)(2,1)S(1)}, u32[]{:S(2)}, u32[]{:S(2)}) async-start(bf16[128,16,224]{0,2,1:T(8,128)(2,1)} %bitcast.52), calls=%async_computation.1 | async-start | bytes 1835008 | tf_op jit(solution)/shard_map/all_to_all | solution.py:50
  212.4 131.7 %reduce-scatter.3.cloned.1.call-start = ((), (), s32[]{:S(2)}) async-start(), calls=%async_computation.5 | async-start | bytes 25165824 | tf_op jit(solution)/shard_map/reduce_scatter | solution.py:77
  236.2 14.8 %copy-start.11 = (bf16[224,2048]{1,0:T(8,128)(2,1)}, bf16[224,2048]{1,0:T(8,128)(2,1)S(1)}, u32[]{:S(2)}) copy-start(bf16[224,2048]{1,0:T(8,128)(2,1)S(1)} %get-tuple-element.64) | copy-start | bytes 2752516
  257.8 8.4 %copy-start.12 = (bf16[2,2048,2048]{2,1,0:T(8,128)(2,1)S(1)}, bf16[2,2048,2048]{2,1,0:T(8,128)(2,1)}, u32[]{:S(2)}) copy-start(bf16[2,2048,2048]{2,1,0:T(8,128)(2,1)} %all-gather.2.cloned.1.call-done) | copy-start | bytes 50331652
  266.2 5.2 copy-start.10
  285.7 15.0 %copy-start.3 = (bf16[2048,224]{0,1:T(8,128)(2,1)}, bf16[2048,224]{0,1:T(8,128)(2,1)S(1)}, u32[]{:S(2)}) copy-start(bf16[2048,224]{0,1:T(8,128)(2,1)S(1)} %get-tuple-element.12) | copy-start | bytes 2752516
  317.7 220.3 %reduce-scatter.5.cloned.1.call-start = ((), (), s32[]{:S(2)}) async-start(), calls=%async_computation.6 | async-start | bytes 8912896 | tf_op jit(solution)/shard_map/reduce_scatter | solution.py:80
  345.2 8.0 %copy-start.4 = (bf16[2048,224]{0,1:T(8,128)(2,1)S(1)}, bf16[2048,224]{0,1:T(8,128)(2,1)}, u32[]{:S(2)}) copy-start(bf16[2048,224]{0,1:T(8,128)(2,1)} %copy-done.3) | copy-start | bytes 2752516
  346.3 41.1 %all-to-all-start = ((bf16[16,128,224]{1,2,0:T(8,128)(2,1)}), bf16[16,128,224]{1,2,0:T(8,128)(2,1)S(1)}, u32[]{:S(2)}, u32[]{:S(2)}) async-start(bf16[16,128,224]{1,2,0:T(8,128)(2,1)} %bitcast.117), calls=%async_computation | async-start | bytes 1835008 | tf_op jit(solution)/shard_map/all_to_all | solution.py:74
  353.2 11.6 %slice-start = ((s8[16777216]{0:T(1024)(128)(4,1)}), s8[4194304]{0:T(1024)(128)(4,1)S(1)}, s32[]{:S(2)}) async-start(s8[16777216]{0:T(1024)(128)(4,1)} %bitcast.151), calls=%async_computation.7 | async-start | bytes 8388608
  353.2 11.6 %slice-start.1 = ((s8[16777216]{0:T(1024)(128)(4,1)}), s8[4194304]{0:T(1024)(128)(4,1)S(1)}, s32[]{:S(2)}) async-start(s8[16777216]{0:T(1024)(128)(4,1)} %bitcast.151), calls=%async_computation.8 | async-start | bytes 8388608
  359.2 5.6 %slice-start.2 = ((s8[16777216]{0:T(1024)(128)(4,1)}), s8[4194304]{0:T(1024)(128)(4,1)S(1)}, s32[]{:S(2)}) async-start(s8[16777216]{0:T(1024)(128)(4,1)} %bitcast.151), calls=%async_computation.9 | async-start | bytes 8388608
  359.2 5.8 %slice-start.3 = ((s8[16777216]{0:T(1024)(128)(4,1)}), s8[4194304]{0:T(1024)(128)(4,1)S(1)}, s32[]{:S(2)}) async-start(s8[16777216]{0:T(1024)(128)(4,1)} %bitcast.151), calls=%async_computation.10 | async-start | bytes 8388608
  (5 other events, 5.1 us)
Sparse Core Ops, SparseCore 0:
  192.6 39.5 all-gather.1
  317.8 26.1 reduce-scatter.2
  346.9 191.0 reduce-scatter.4
